TPU v7x, 256 devices: a whole 4x4x8 slice. The times are simulated.
256 devices in a mesh: seq: 128 (over x, y, z), head: 2 (over core).
Axes of the slice: x: 4, y: 4, z: 8, core: 2. Of those that a mesh axis runs over, the one named last changes fastest.
Arguments:
- tiles: bfloat16 [16384, 768], P('seq', 'head'), may hold values from -6 to 6
- ln_gain: float32 [768], replicated, may hold values from 0.25 to 1.75
- w_qkv: bfloat16 [768, 3, 768], P(None, None, 'head'), as said below
- w_out: bfloat16 [768, 768], P('head'), may hold values from -0.21875 to 0.21875
- tile_source: int32 [16384], P('seq'), may hold values from 0 to 16383, as said below
- tissue_count: int32 [128], P('seq'), may hold values from 64 to 128
Outputs:
- encoded: bfloat16 [16384, 768], P('seq', 'head')
Inputs may be any that keep to these rules, and one draw needn't show every extreme that they name: `tile_source`: A permutation of the 16384 rows; exactly one tile goes to Hilbert block d from each encoder block s, namely row s * 128 + d; within block d these 128 tiles come in any order. `w_qkv`: projection weights; the query third may be larger than the key and value thirds.
All inputs are finite; a program needn't handle non-finite values.
Results may differ from a plain program's by a relative error of at most 0.0095.
The roundings to bfloat16 on the way count: a program that leaves them out, or rounds other values in their place, can miss the bound.
Values may be sent and summed in bfloat16 or wider, within the bound.
A program may use at most 64 MiB of HBM per device.

v0:
```python
import jax
import jax.numpy as jnp
from jax import lax
from jax.sharding import PartitionSpec as P

D = 768
HEAD_DIM = 64
SPAN_SHORT = 4
MIDDLE_SPAN = 16
MIDDLE_DILATION = 4
WHOLE_DILATION = 16
masked_score = -1e30


def shortened(value):

    def short(part):
        return part.astype(jnp.bfloat16) if part.dtype == jnp.float32 else part

    return jax.tree.map(short, value)


def swapped(value, axis, apart):
    return lax.ppermute(value, axis, [(i, i ^ 1 << apart) for i in range(lax.axis_size(axis))])


def absorb(softmax_state, queries, key_matrix, value_matrix, key_live):
    running_max, running_sum, weighted = softmax_state
    scores = jnp.einsum(
        "qhd,khd->hqk", queries, key_matrix, preferred_element_type=jnp.float32
    ) * queries.shape[-1] ** (-0.5)
    scores = jnp.where(key_live.T[:, None, :] > 0.5, scores, masked_score)
    new_max = jnp.maximum(running_max, jnp.max(scores, axis=-1))
    rescale = jnp.exp(running_max - new_max)
    probability = jnp.exp(scores - new_max[..., None])
    running_sum = running_sum * rescale + jnp.sum(probability, axis=-1)
    mixed = jnp.einsum(
        "hqk,khd->qhd",
        probability.astype(jnp.bfloat16),
        value_matrix,
        preferred_element_type=jnp.float32,
    )
    weighted = weighted * rescale.T[:, :, None] + mixed
    return (new_max, running_sum, weighted)


def select_rows(key_matrix, value_matrix, row_active_mask, stride, offsets):
    kept_rows = key_matrix.shape[0] // stride
    heads_local = key_matrix.shape[1]
    selector = jnp.broadcast_to(
        offsets[None, None, :, None], (kept_rows, 1, heads_local, key_matrix.shape[2])
    )
    picked_keys = jnp.take_along_axis(
        key_matrix.reshape(kept_rows, stride, heads_local, key_matrix.shape[2]), selector, axis=1
    )[:, 0]
    picked_values = jnp.take_along_axis(
        value_matrix.reshape(kept_rows, stride, heads_local, value_matrix.shape[2]),
        selector,
        axis=1,
    )[:, 0]
    picked_live = row_active_mask.reshape(kept_rows, stride)[:, offsets]
    return (picked_keys, picked_values, picked_live)


def join_parts(local_part, remote_part):
    return tuple(
        (
            jnp.concatenate((mine_rows, their_rows), 0)
            for mine_rows, their_rows in zip(local_part, remote_part)
        )
    )


def absorb_blocks(softmax_state, queries, members, step_rows):
    for offset_row in range(0, members[0].shape[0], step_rows):
        softmax_state = absorb(
            softmax_state,
            queries,
            *[member[offset_row : offset_row + step_rows] for member in members]
        )
    return softmax_state


def shards(tiles, ln_gain, w_qkv, w_out, tile_source, tissue_count):
    tok_rows = tiles.shape[0]
    blocks = lax.axis_size("seq")
    per_peer = tok_rows // blocks
    arrival = tile_source // tok_rows * per_peer + tile_source % per_peer
    whole_rows = lax.all_gather(tiles, "head", axis=1, tiled=True)
    arrived = lax.all_to_all(
        whole_rows.reshape(blocks, per_peer, whole_rows.shape[1]),
        "seq",
        split_axis=0,
        concat_axis=0,
        tiled=True,
    )
    relaid = arrived.reshape(tok_rows, whole_rows.shape[1])[arrival]
    widened = relaid.astype(jnp.float32)
    row_mean = jnp.mean(widened, axis=-1, keepdims=True)
    centered = widened - row_mean
    row_var = jnp.mean(centered * centered, axis=-1, keepdims=True)
    normed = (centered * lax.rsqrt(row_var + 1e-05) * ln_gain).astype(jnp.bfloat16)
    heads_local = w_qkv.shape[2] // HEAD_DIM
    packed = jnp.dot(
        normed, w_qkv.reshape(D, 3 * w_qkv.shape[2]), preferred_element_type=jnp.float32
    ).astype(jnp.bfloat16)
    packed = packed.reshape(tok_rows, 3, heads_local, HEAD_DIM)
    queries, key_matrix, value_matrix = (packed[:, 0], packed[:, 1], packed[:, 2])
    row_active_mask = (jnp.arange(tok_rows, dtype=jnp.int32) < tissue_count[0]).astype(jnp.bfloat16)
    live_all = jnp.broadcast_to(row_active_mask[:, None], (tok_rows, heads_local))
    present_heads = lax.axis_index("head") * heads_local + jnp.arange(heads_local, dtype=jnp.int32)
    softmax_state = (
        jnp.full((heads_local, tok_rows), masked_score, jnp.float32),
        jnp.zeros((heads_local, tok_rows), jnp.float32),
        jnp.zeros((tok_rows, heads_local, HEAD_DIM), jnp.float32),
    )
    gathered = (key_matrix, value_matrix, live_all)
    for level in range(SPAN_SHORT.bit_length() - 1):
        partner = jax.tree.map(
            lambda part, own: part.astype(own.dtype),
            swapped(shortened(gathered), "seq", level),
            gathered,
        )
        gathered = join_parts(gathered, partner)
    softmax_state = absorb(softmax_state, queries, *gathered)
    middle_branch = select_rows(
        key_matrix, value_matrix, row_active_mask, MIDDLE_DILATION, present_heads % MIDDLE_DILATION
    )
    faraway_part = select_rows(
        key_matrix, value_matrix, row_active_mask, WHOLE_DILATION, present_heads % WHOLE_DILATION
    )
    for level in range(MIDDLE_SPAN.bit_length() - 1):
        partner = jax.tree.map(
            lambda part, own: part.astype(own.dtype),
            swapped(shortened(middle_branch), "seq", level),
            middle_branch,
        )
        middle_branch = join_parts(middle_branch, partner)
    softmax_state = absorb(softmax_state, queries, *middle_branch)
    faraway_part = (
        lax.all_gather(faraway_part[0], "seq", axis=0, tiled=True),
        lax.all_gather(faraway_part[1], "seq", axis=0, tiled=True),
        lax.all_gather(faraway_part[2], "seq", axis=0, tiled=True),
    )
    step_rows = min(faraway_part[0].shape[0], middle_branch[0].shape[0])
    softmax_state = absorb_blocks(softmax_state, queries, faraway_part, step_rows)
    running_max, running_sum, weighted = softmax_state
    attended = (
        weighted / running_sum.T[:, :, None] * row_active_mask.astype(jnp.float32)[:, None, None]
    )
    attended = attended.astype(jnp.bfloat16).reshape(tok_rows, heads_local * HEAD_DIM)
    partial_value = jnp.dot(attended, w_out, preferred_element_type=jnp.float32)
    return lax.psum_scatter(
        partial_value.astype(jnp.bfloat16), "head", scatter_dimension=1, tiled=True
    )


def solution(mesh):
    return jax.shard_map(
        shards,
        mesh=mesh,
        in_specs=(
            P("seq", "head"),
            P(),
            P(None, None, "head"),
            P("head", None),
            P("seq"),
            P("seq"),
        ),
        out_specs=P("seq", "head"),
        check_vma=False,
    )
```

profile of v0, /device:TPU:1, one launch (start us, length us, event | category | flops | bytes accessed | tf_op | source)
XLA Modules:
  0.0 1479.4 jit_solution(4829713266391347686)
XLA Ops:
  6.5 5.3 all_gather.12
  11.8 0.5 broadcast.579
  12.4 0.7 reduce
  13.1 0.7 reshape.331
  13.8 13.8 all-to-all-start
  28.3 0.6 gather_fusion.1
  28.9 0.7 collective-permute-start.6
  29.6 0.9 collective-permute-start
  31.2 0.6 gather_fusion.2
  31.8 290.8 %all-gather = bf16[1024,6]{1,0:T(8,128)(2,1)S(1)} all-gather(bf16[8,6]{1,0:T(8,128)(2,1)S(1)} %copy.105), channel_id=2, replica_groups=mesh['seq'=128,'head'=2] {'seq'}, dimensions={0}, use_global_device_ids=true | all-gather | bytes 12384 | tf_op jit(solution)/shard_map/all_gather | solution.py:143
  323.2 2.6 copy.90
  326.5 2.1 collective-permute-start.1
  328.6 4.2 collective-permute-done.8
  332.9 2.7 collective-permute-done.9
  335.9 0.9 gather_fusion
  337.1 0.7 convolution_convert_fusion
  338.4 130.2 %gather_fusion.3 = bf16[12288]{0:T(1024)(128)(2,1)S(1)} fusion(bf16[32,4,6,64]{3,1,0,2:T(4,128)(2,1)S(1)} %bitcast.224, s32[12288]{0:T(1024)S(1)} %reshape.307), kind=kCustom, calls=%fused_computation.clone | custom fusion | bytes 245760 | tf_op jit(solution)/shard_map/jit(take_along_axis)/gather | solution.py:53
  468.9 130.2 %gather_fusion.4 = bf16[12288]{0:T(1024)(128)(2,1)S(1)} fusion(bf16[32,4,6,64]{3,1,0,2:T(4,128)(2,1)S(1)} %bitcast.226, s32[12288]{0:T(1024)S(1)} %reshape.313), kind=kCustom, calls=%fused_computation.2.clone | custom fusion | bytes 245760 | tf_op jit(solution)/shard_map/jit(take_along_axis)/gather | solution.py:56
  599.2 0.7 constant_dynamic-update-slice_fusion.9
  600.0 33.9 %gather_fusion.5 = bf16[3072]{0:T(1024)(128)(2,1)S(1)} fusion(bf16[8,16,6,64]{3,1,0,2:T(8,128)(2,1)S(1)} %bitcast.225, s32[3072]{0:T(1024)S(1)} %reshape.319), kind=kCustom, calls=%fused_computation.1.clone | custom fusion | bytes 61440 | tf_op jit(solution)/shard_map/jit(take_along_axis)/gather | solution.py:53
  633.9 33.9 %gather_fusion.6 = bf16[3072]{0:T(1024)(128)(2,1)S(1)} fusion(bf16[8,16,6,64]{3,1,0,2:T(8,128)(2,1)S(1)} %bitcast.227, s32[3072]{0:T(1024)S(1)} %reshape.319), kind=kCustom, calls=%fused_computation.3.clone | custom fusion | bytes 61440 | tf_op jit(solution)/shard_map/jit(take_along_axis)/gather | solution.py:56
  668.0 292.7 %all-gather.1 = bf16[1024,1,6,64]{3,0,2,1:T(8,128)(2,1)S(1)} all-gather(bf16[8,1,6,64]{3,0,2,1:T(8,128)(2,1)S(1)} %copy.110), channel_id=3, replica_groups=mesh['seq'=128,'head'=2] {'seq'}, dimensions={0}, use_global_device_ids=true | all-gather | bytes 792576 | tf_op jit(solution)/shard_map/all_gather | solution.py:141
  960.7 1.5 collective-permute-start.14
  962.2 291.3 %all-gather.2 = bf16[1024,1,6,64]{3,0,2,1:T(8,128)(2,1)S(1)} all-gather(bf16[8,1,6,64]{3,0,2,1:T(8,128)(2,1)S(1)} %copy.115), channel_id=4, replica_groups=mesh['seq'=128,'head'=2] {'seq'}, dimensions={0}, use_global_device_ids=true | all-gather | bytes 792576 | tf_op jit(solution)/shard_map/all_gather | solution.py:142
  1253.5 0.5 fusion.107
  1254.0 0.5 fusion.106
  1254.5 1.7 collective-permute-start.4
  1256.4 2.4 collective-permute-start.15
  1258.8 6.0 collective-permute-done.11
  1265.0 0.9 collective-permute-done.15
  1265.9 4.5 collective-permute-start.16
  1270.7 2.4 collective-permute-start.5
  1273.1 0.6 collective-permute-done.12
  1273.9 3.3 collective-permute-done.16
  1277.6 2.4 collective-permute-done.3
  1280.8 0.5 fusion.1
  1281.3 0.5 fusion.2
  1281.9 0.6 convolution_bitcast_fusion.2
  1282.4 0.5 fusion.4
  1283.0 0.6 convolution_bitcast_fusion.1
  1283.6 0.5 fusion.8
  1284.1 0.6 collective-permute-done.17
  1284.7 0.7 convolution_bitcast_fusion.3
  1285.4 0.5 fusion.6
  1286.0 0.6 fusion.19
  1286.8 0.8 copy.122
  1287.7 183.2 %reduce-scatter.4.cloned.1.call-done = bf16[384,128]{1,0:T(8,128)(2,1)} async-done(((bf16[768,128]{1,0:T(8,128)(2,1)}), bf16[384,128]{1,0:T(8,128)(2,1)}) %reduce-scatter.4.cloned.1.call-update) | async-done | bytes 98320
  1470.9 1.6 copy.123
  (118 shorter events, 6.0 us)
Async XLA Ops:
  6.5 1280.0 %copy-start = (bf16[384,768]{1,0:T(8,128)(2,1)S(1)}, bf16[384,768]{1,0:T(8,128)(2,1)}, u32[]{:S(2)}) copy-start(bf16[384,768]{1,0:T(8,128)(2,1)} %param.13) | copy-start | bytes 1769476
  11.8 18.9 %copy-start.3 = (s32[128]{0:T(128)S(1)}, s32[128]{0:T(128)}, u32[]{:S(2)}) copy-start(s32[128]{0:T(128)} %param.14) | copy-start | bytes 1540
  13.8 321.9 %all-to-all-start = ((bf16[128,2,384]{2,1,0:T(2,128)(2,1)}), bf16[128,2,384]{2,1,0:T(2,128)(2,1)S(1)}, u32[]{:S(2)}, u32[]{:S(2)}) async-start(bf16[128,2,384]{2,1,0:T(2,128)(2,1)} %reshape.331), calls=%async_computation | async-start | bytes 393216 | tf_op jit(solution)/shard_map/all_to_all | solution.py:90
  27.6 1443.3 %reduce-scatter.4.cloned.1.call-start = ((), (), s32[]{:S(2)}) async-start(), calls=%async_computation.2 | async-start | bytes 294912
  28.9 294.0 %collective-permute-start.6 = (bf16[32,6]{0,1:T(8,128)(2,1)S(1)}, bf16[32,6]{0,1:T(8,128)(2,1)S(1)}, u32[]{:S(2)}, u32[]{:S(2)}) collective-permute-start(bf16[32,6]{0,1:T(8,128)(2,1)S(1)} %bitcast.237), channel_id=1, source_target_pairs={{0,2},{2,0},{4,6},{6,4},{8,10},{10,8},{12,14},{14,12},{16,18},{18,... | collective-permute-start | bytes 1160 | tf_op jit(solution)/shard_map/ppermute | solution.py:24
  29.6 296.9 %collective-permute-start = (bf16[128,6]{0,1:T(8,128)(2,1)S(1)}, bf16[128,6]{0,1:T(8,128)(2,1)S(1)}, u32[]{:S(2)}, u32[]{:S(2)}) collective-permute-start(bf16[128,6]{0,1:T(8,128)(2,1)S(1)} %broadcast_in_dim.86), channel_id=1, source_target_pairs={{0,2},{2,0},{4,6},{6,4},{8,10},{10,8},{12,14},{14,12},{16,18},{18,... | collective-permute-start | bytes 4616 | tf_op jit(solution)/shard_map/ppermute | solution.py:24
  323.0 3.4 collective-permute-start.7
  326.4 6.4 collective-permute-start.8
  326.5 6.4 collective-permute-start.1
  332.8 2.8 collective-permute-start.9
  335.7 1.4 copy-start.1
  600.0 656.2 %collective-permute-start.10 = (bf16[32,6,64]{2,0,1:T(8,128)(2,1)S(1)}, bf16[32,6,64]{2,0,1:T(8,128)(2,1)S(1)}, u32[]{:S(2)}, u32[]{:S(2)}) collective-permute-start(bf16[32,6,64]{2,0,1:T(8,128)(2,1)S(1)} %get-tuple-element.27), channel_id=1, source_target_pairs={{0,2},{2,0},{4,6},{6,4},{8,10},{10,8},{12,14},{14,12},{16,18},{18,... | collective-permute-start | bytes 73736 | tf_op jit(solution)/shard_map/ppermute | solution.py:24
  960.7 309.8 %collective-permute-start.2 = (bf16[128,6,64]{0,2,1:T(8,128)(2,1)S(1)}, bf16[128,6,64]{0,2,1:T(8,128)(2,1)S(1)}, u32[]{:S(2)}, u32[]{:S(2)}) collective-permute-start(bf16[128,6,64]{0,2,1:T(8,128)(2,1)S(1)} %get-tuple-element.18), channel_id=1, source_target_pairs={{0,2},{2,0},{4,6},{6,4},{8,10},{10,8},{12,14},{14,12},{16,18},{18,... | collective-permute-start | bytes 294920 | tf_op jit(solution)/shard_map/ppermute | solution.py:24
  960.7 295.6 %collective-permute-start.14 = (bf16[32,6,64]{2,0,1:T(8,128)(2,1)S(1)}, bf16[32,6,64]{2,0,1:T(8,128)(2,1)S(1)}, u32[]{:S(2)}, u32[]{:S(2)}) collective-permute-start(bf16[32,6,64]{2,0,1:T(8,128)(2,1)S(1)} %get-tuple-element.11), channel_id=1, source_target_pairs={{0,2},{2,0},{4,6},{6,4},{8,10},{10,8},{12,14},{14,12},{16,18},{18,... | collective-permute-start | bytes 73736 | tf_op jit(solution)/shard_map/ppermute | solution.py:24
  1254.0 4.8 copy-start.2
  1254.5 16.1 %collective-permute-start.4 = (bf16[128,6,64]{0,2,1:T(8,128)(2,1)S(1)}, bf16[128,6,64]{0,2,1:T(8,128)(2,1)S(1)}, u32[]{:S(2)}, u32[]{:S(2)}) collective-permute-start(bf16[128,6,64]{0,2,1:T(8,128)(2,1)S(1)} %get-tuple-element.17), channel_id=1, source_target_pairs={{0,2},{2,0},{4,6},{6,4},{8,10},{10,8},{12,14},{14,12},{16,18},{18,... | collective-permute-start | bytes 294920 | tf_op jit(solution)/shard_map/ppermute | solution.py:24
  1256.2 8.6 collective-permute-start.11
  1256.4 9.5 collective-permute-start.15
  1264.9 8.8 collective-permute-start.12
  1265.9 11.2 collective-permute-start.16
  1270.5 9.5 collective-permute-start.3
  1270.7 15.3 %collective-permute-start.5 = (bf16[256,6,64]{0,2,1:T(8,128)(2,1)S(1)}, bf16[256,6,64]{0,2,1:T(8,128)(2,1)S(1)}, u32[]{:S(2)}, u32[]{:S(2)}) collective-permute-start(bf16[256,6,64]{0,2,1:T(8,128)(2,1)S(1)} %pad_maximum_fusion.3), channel_id=1, source_target_pairs={{0,4},{2,6},{4,0},{6,2},{8,12},{10,14},{12,8},{14,10},{16,20},{18,... | collective-permute-start | bytes 589832 | tf_op jit(solution)/shard_map/ppermute | solution.py:24
  1273.8 7.0 collective-permute-start.13
  1277.2 7.5 collective-permute-start.17
Sparse Core Ops, SparseCore 0:
  1287.8 183.0 reduce-scatter.3
where the time goes:
time: 1480 us
  blocking collectives  880 us (59%)
  local copies, waits for them, and re-layouts  339 us (23%)
  waiting for transfers between devices  204 us (14%)
  starting transfers between devices  30.8 us (2%)
    all_gather x1, blocking collectives, shards(): lax.all_gather(faraway_part[0], 'seq', axis=0, tiled=True)  293 us
    all_gather x1, blocking collectives, shards(): lax.all_gather(faraway_part[1], 'seq', axis=0, tiled=True)  291 us
    all_gather x1, blocking collectives, shards(): lax.all_gather(faraway_part[2], 'seq', axis=0, tiled=True)  291 us
    unnamed x2, waiting for transfers between devices  183 us
    gather x8, local copies, waits for them, and re-layouts, select_rows(): jnp.take_along_axis(key_matrix.reshape(kept_rows, stride, heads_local, ke...  165 us
    gather x6, local copies, waits for them, and re-layouts, select_rows(): jnp.take_along_axis(value_matrix.reshape(kept_rows, stride, heads_local,...  164 us
  transfers between devices with their start and end apart: 20, of which 11 were waited for; matrix products, arithmetic and copies ran while one was open for 5% of the time, Pallas kernels for 0%

commit v1 on v0

--- a/solution.py
+++ b/solution.py
@@ -2,6 +2,7 @@
 import jax.numpy as jnp
 from jax import lax
 from jax.sharding import PartitionSpec as P
+from jax.lax import all_to_all, axis_size
 
 D = 768
 HEAD_DIM = 64
@@ -137,9 +138,12 @@
         )
         middle_branch = join_parts(middle_branch, partner)
     softmax_state = absorb(softmax_state, queries, *middle_branch)
+    play_copies_over_axis = lambda sheet: jnp.concatenate(
+        all_to_all(jnp.stack([sheet for _ in range(axis_size("seq"))], axis=0), "seq", 0, 0), axis=0
+    )
     faraway_part = (
         lax.all_gather(faraway_part[0], "seq", axis=0, tiled=True),
-        lax.all_gather(faraway_part[1], "seq", axis=0, tiled=True),
+        play_copies_over_axis(faraway_part[1]),
         lax.all_gather(faraway_part[2], "seq", axis=0, tiled=True),
     )
     step_rows = min(faraway_part[0].shape[0], middle_branch[0].shape[0])

time: 1480 us -> 1170 us (0.79)
  blocking collectives: 880 us -> 589 us
  waiting for transfers between devices: 204 us -> 151 us
    all_gather x1 -> x0, blocking collectives: 291 us -> none  [shards(): lax.all_gather(faraway_part[1], 'seq', axis=0, tiled=True)]
    unnamed x2, waiting for transfers between devices: 183 us -> 132 us
  transfers between devices with their start and end apart: 20 -> 21, of which waited for: 11 -> 6; matrix products, arithmetic and copies ran while one was open for 5% -> 8% of each run, Pallas kernels for 0% -> 0%
where the time goes in v1:
time: 1170 us
  blocking collectives  589 us (50%)
  local copies, waits for them, and re-layouts  353 us (30%)
  waiting for transfers between devices  151 us (13%)
  starting transfers between devices  41.8 us (4%)
  between operations  14.7 us (1%)
    all_gather x1, blocking collectives, shards(): lax.all_gather(faraway_part[0], 'seq', axis=0, tiled=True)  293 us
    all_gather x1, blocking collectives, shards(): lax.all_gather(faraway_part[2], 'seq', axis=0, tiled=True)  291 us
    gather x8, local copies, waits for them, and re-layouts, select_rows(): jnp.take_along_axis(key_matrix.reshape(kept_rows, stride, heads_local, ke...  165 us
    gather x6, local copies, waits for them, and re-layouts, select_rows(): jnp.take_along_axis(value_matrix.reshape(kept_rows, stride, heads_local,...  164 us
    unnamed x2, waiting for transfers between devices  132 us
  transfers between devices with their start and end apart: 21, of which 6 were waited for; matrix products, arithmetic and copies ran while one was open for 8% of the time, Pallas kernels for 0%

profile of v1, /device:TPU:1, one launch (start us, length us, event | category | flops | bytes accessed | tf_op | source)
XLA Modules:
  0.0 1166.7 jit_solution(10491500510538169196)
XLA Ops:
  6.5 5.3 all_gather.9
  12.4 0.7 reduce
  13.1 0.7 reshape.333
  13.8 13.8 %all-to-all-start = ((bf16[128,2,384]{2,1,0:T(2,128)(2,1)}), bf16[128,2,384]{2,1,0:T(2,128)(2,1)S(1)}, u32[]{:S(2)}, u32[]{:S(2)}) async-start(bf16[128,2,384]{2,1,0:T(2,128)(2,1)} %reshape.333), calls=%async_computation | async-start | bytes 393216 | tf_op jit(solution)/shard_map/all_to_all | solution.py:91
  28.9 0.7 collective-permute-start.6
  29.5 0.9 collective-permute-start
  31.9 290.8 %all-gather = bf16[1024,6]{1,0:T(8,128)(2,1)S(1)} all-gather(bf16[8,6]{1,0:T(8,128)(2,1)S(1)} %copy.115), channel_id=2, replica_groups=mesh['seq'=128,'head'=2] {'seq'}, dimensions={0}, use_global_device_ids=true | all-gather | bytes 12384 | tf_op jit(solution)/shard_map/all_gather | solution.py:147
  324.4 2.6 copy.100
  327.4 2.4 collective-permute-start.1
  329.9 3.9 collective-permute-done.8
  333.9 2.7 collective-permute-done.9
  336.9 0.9 gather_fusion
  338.1 0.7 convolution_convert_fusion
  339.1 0.7 slice_bitcast_fusion.9
  340.0 130.2 %gather_fusion.3 = bf16[12288]{0:T(1024)(128)(2,1)S(1)} fusion(bf16[32,4,6,64]{3,1,0,2:T(4,128)(2,1)S(1)} %bitcast.227, s32[12288]{0:T(1024)S(1)} %reshape.309), kind=kCustom, calls=%fused_computation.clone | custom fusion | bytes 245760 | tf_op jit(solution)/shard_map/jit(take_along_axis)/gather | solution.py:54
  470.5 130.2 %gather_fusion.4 = bf16[12288]{0:T(1024)(128)(2,1)S(1)} fusion(bf16[32,4,6,64]{3,1,0,2:T(4,128)(2,1)S(1)} %bitcast.229, s32[12288]{0:T(1024)S(1)} %reshape.315), kind=kCustom, calls=%fused_computation.2.clone | custom fusion | bytes 245760 | tf_op jit(solution)/shard_map/jit(take_along_axis)/gather | solution.py:57
  600.9 0.8 constant_dynamic-update-slice_fusion.9
  601.7 33.9 %gather_fusion.5 = bf16[3072]{0:T(1024)(128)(2,1)S(1)} fusion(bf16[8,16,6,64]{3,1,0,2:T(8,128)(2,1)S(1)} %bitcast.228, s32[3072]{0:T(1024)S(1)} %reshape.321), kind=kCustom, calls=%fused_computation.1.clone | custom fusion | bytes 61440 | tf_op jit(solution)/shard_map/jit(take_along_axis)/gather | solution.py:54
  635.7 33.9 %gather_fusion.6 = bf16[3072]{0:T(1024)(128)(2,1)S(1)} fusion(bf16[8,16,6,64]{3,1,0,2:T(8,128)(2,1)S(1)} %bitcast.230, s32[3072]{0:T(1024)S(1)} %reshape.321), kind=kCustom, calls=%fused_computation.3.clone | custom fusion | bytes 61440 | tf_op jit(solution)/shard_map/jit(take_along_axis)/gather | solution.py:57
  669.8 292.6 %all-gather.1 = bf16[1024,1,6,64]{3,0,2,1:T(8,128)(2,1)S(1)} all-gather(bf16[8,1,6,64]{3,0,2,1:T(8,128)(2,1)S(1)} %copy.120), channel_id=3, replica_groups=mesh['seq'=128,'head'=2] {'seq'}, dimensions={0}, use_global_device_ids=true | all-gather | bytes 792576 | tf_op jit(solution)/shard_map/all_gather | solution.py:145
  962.4 1.6 fusion.111
  964.6 1.5 collective-permute-start.14
  966.0 1.3 broadcast_bitcast_fusion
  967.4 3.8 reshape.335
  971.2 6.2 all-to-all-start.1
  978.0 2.2 collective-permute-start.11
  981.8 6.4 collective-permute-done.11
  988.2 4.1 collective-permute-start.12
  992.4 3.2 collective-permute-start.16
  995.6 0.7 constant_dynamic-update-slice_fusion.2
  996.3 0.7 constant_dynamic-update-slice_fusion.7
  996.9 1.0 pad_maximum_fusion.2
  998.0 0.9 collective-permute-start.3
  998.9 0.7 pad_maximum_fusion.3
  999.6 1.5 collective-permute-start.5
  1001.2 1.3 collective-permute-start.13
  1003.2 2.1 collective-permute-start.17
  1005.4 6.1 collective-permute-done.3
  1011.5 1.4 fusion
  1013.6 1.3 copy-done.1
  1017.0 1.4 convolution_bitcast_fusion.3
  1018.3 1.9 reshape.336
  1020.2 1.6 fusion.108
  1023.3 0.8 copy-done.4
  1024.1 1.5 fusion.19
  1025.9 0.8 copy.136
  1026.7 131.5 %reduce-scatter.4.cloned.1.call-done = bf16[384,128]{1,0:T(8,128)(2,1)} async-done(((bf16[768,128]{1,0:T(8,128)(2,1)}), bf16[384,128]{1,0:T(8,128)(2,1)}) %reduce-scatter.4.cloned.1.call-update) | async-done | bytes 98320
  1158.2 1.6 copy.137
  (155 shorter events, 14.5 us)
Async XLA Ops:
  6.5 1019.1 %copy-start = (bf16[384,768]{1,0:T(8,128)(2,1)S(1)}, bf16[384,768]{1,0:T(8,128)(2,1)}, u32[]{:S(2)}) copy-start(bf16[384,768]{1,0:T(8,128)(2,1)} %param.13) | copy-start | bytes 1769476
  11.8 18.9 %copy-start.17 = (s32[128]{0:T(128)S(1)}, s32[128]{0:T(128)}, u32[]{:S(2)}) copy-start(s32[128]{0:T(128)} %param.14) | copy-start | bytes 1540
  13.8 322.9 %all-to-all-start = ((bf16[128,2,384]{2,1,0:T(2,128)(2,1)}), bf16[128,2,384]{2,1,0:T(2,128)(2,1)S(1)}, u32[]{:S(2)}, u32[]{:S(2)}) async-start(bf16[128,2,384]{2,1,0:T(2,128)(2,1)} %reshape.333), calls=%async_computation | async-start | bytes 393216 | tf_op jit(solution)/shard_map/all_to_all | solution.py:91
  28.9 294.7 %collective-permute-start.6 = (bf16[32,6]{0,1:T(8,128)(2,1)S(1)}, bf16[32,6]{0,1:T(8,128)(2,1)S(1)}, u32[]{:S(2)}, u32[]{:S(2)}) collective-permute-start(bf16[32,6]{0,1:T(8,128)(2,1)S(1)} %bitcast.241), channel_id=1, source_target_pairs={{0,2},{2,0},{4,6},{6,4},{8,10},{10,8},{12,14},{14,12},{16,18},{18,... | collective-permute-start | bytes 1160 | tf_op jit(solution)/shard_map/ppermute | solution.py:25
  29.5 297.9 %collective-permute-start = (bf16[128,6]{0,1:T(8,128)(2,1)S(1)}, bf16[128,6]{0,1:T(8,128)(2,1)S(1)}, u32[]{:S(2)}, u32[]{:S(2)}) collective-permute-start(bf16[128,6]{0,1:T(8,128)(2,1)S(1)} %broadcast_in_dim.86), channel_id=1, source_target_pairs={{0,2},{2,0},{4,6},{6,4},{8,10},{10,8},{12,14},{14,12},{16,18},{18,... | collective-permute-start | bytes 4616 | tf_op jit(solution)/shard_map/ppermute | solution.py:25
  30.4 0.5 copy-start.11
  30.5 0.6 copy-start.13
  30.5 0.6 copy-start.15
  323.6 3.7 collective-permute-start.7
  327.4 6.4 collective-permute-start.8
  327.4 6.5 collective-permute-start.1
  333.9 2.8 collective-permute-start.9
  336.7 1.4 copy-start.9
  601.7 376.3 %collective-permute-start.10 = (bf16[32,6,64]{2,0,1:T(8,128)(2,1)S(1)}, bf16[32,6,64]{2,0,1:T(8,128)(2,1)S(1)}, u32[]{:S(2)}, u32[]{:S(2)}) collective-permute-start(bf16[32,6,64]{2,0,1:T(8,128)(2,1)S(1)} %get-tuple-element.29), channel_id=1, source_target_pairs={{0,2},{2,0},{4,6},{6,4},{8,10},{10,8},{12,14},{14,12},{16,18},{18,... | collective-permute-start | bytes 73736 | tf_op jit(solution)/shard_map/ppermute | solution.py:25
  635.6 34.0 %copy-start.12 = (s32[6]{0:T(128)S(1)}, s32[6]{0:T(128)}, u32[]{:S(2)}) copy-start(s32[6]{0:T(128)} %copy-done.11) | copy-start | bytes 76
  635.7 34.0 %copy-start.14 = (s32[6]{0:T(128)S(1)}, s32[6]{0:T(128)}, u32[]{:S(2)}) copy-start(s32[6]{0:T(128)} %copy-done.13) | copy-start | bytes 76
  635.7 34.0 %copy-start.16 = (pred[6]{0:T(512)(128)(4,1)S(1)}, pred[6]{0:T(512)(128)(4,1)}, u32[]{:S(2)}) copy-start(pred[6]{0:T(512)(128)(4,1)} %copy-done.15) | copy-start | bytes 22
  962.4 1.6 copy-start.8
  964.5 32.5 %collective-permute-start.2 = (bf16[128,6,64]{0,2,1:T(8,128)(2,1)}, bf16[128,6,64]{0,2,1:T(8,128)(2,1)}, u32[]{:S(2)}, u32[]{:S(2)}) collective-permute-start(bf16[128,6,64]{0,2,1:T(8,128)(2,1)} %get-tuple-element.20), channel_id=1, source_target_pairs={{0,2},{2,0},{4,6},{6,4},{8,10},{10,8},{12,14},{14,12},{16,18},{18,... | collective-permute-start | bytes 294920 | tf_op jit(solution)/shard_map/ppermute | solution.py:25
  964.6 15.6 %collective-permute-start.14 = (bf16[32,6,64]{2,0,1:T(8,128)(2,1)S(1)}, bf16[32,6,64]{2,0,1:T(8,128)(2,1)S(1)}, u32[]{:S(2)}, u32[]{:S(2)}) collective-permute-start(bf16[32,6,64]{2,0,1:T(8,128)(2,1)S(1)} %get-tuple-element.11), channel_id=1, source_target_pairs={{0,2},{2,0},{4,6},{6,4},{8,10},{10,8},{12,14},{14,12},{16,18},{18,... | collective-permute-start | bytes 73736 | tf_op jit(solution)/shard_map/ppermute | solution.py:25
  971.2 47.2 %all-to-all-start.1 = ((bf16[128,2,1536]{2,1,0:T(2,128)(2,1)}), bf16[128,2,1536]{2,1,0:T(2,128)(2,1)S(1)}, u32[]{:S(2)}, u32[]{:S(2)}) async-start(bf16[128,2,1536]{2,1,0:T(2,128)(2,1)} %reshape.335), calls=%async_computation.1 | async-start | bytes 1572864 | tf_op jit(solution)/shard_map/all_to_all | solution.py:142
  977.4 180.9 %reduce-scatter.4.cloned.1.call-start = ((), (), s32[]{:S(2)}) async-start(), calls=%async_computation.3 | async-start | bytes 294912
  977.4 21.5 %collective-permute-start.4 = (bf16[128,6,64]{0,2,1:T(8,128)(2,1)S(1)}, bf16[128,6,64]{0,2,1:T(8,128)(2,1)S(1)}, u32[]{:S(2)}, u32[]{:S(2)}) collective-permute-start(bf16[128,6,64]{0,2,1:T(8,128)(2,1)S(1)} %get-tuple-element.19), channel_id=1, source_target_pairs={{0,2},{2,0},{4,6},{6,4},{8,10},{10,8},{12,14},{14,12},{16,18},{18,... | collective-permute-start | bytes 294920 | tf_op jit(solution)/shard_map/ppermute | solution.py:25
  978.0 10.2 collective-permute-start.11
  980.2 12.2 %collective-permute-start.15 = (bf16[64,6,64]{2,0,1:T(8,128)(2,1)S(1)}, bf16[64,6,64]{2,0,1:T(8,128)(2,1)S(1)}, u32[]{:S(2)}, u32[]{:S(2)}) collective-permute-start(bf16[64,6,64]{2,0,1:T(8,128)(2,1)S(1)} %pad_maximum_fusion.7), channel_id=1, source_target_pairs={{0,4},{2,6},{4,0},{6,2},{8,12},{10,14},{12,8},{14,10},{16,20},{18,... | collective-permute-start | bytes 147464 | tf_op jit(solution)/shard_map/ppermute | solution.py:25
  988.2 12.9 %collective-permute-start.12 = (bf16[128,6,64]{2,0,1:T(8,128)(2,1)S(1)}, bf16[128,6,64]{2,0,1:T(8,128)(2,1)S(1)}, u32[]{:S(2)}, u32[]{:S(2)}) collective-permute-start(bf16[128,6,64]{2,0,1:T(8,128)(2,1)S(1)} %pad_maximum_fusion.4), channel_id=1, source_target_pairs={{0,8},{2,10},{4,12},{6,14},{8,0},{10,2},{12,4},{14,6},{16,24},{18,... | collective-permute-start | bytes 294920 | tf_op jit(solution)/shard_map/ppermute | solution.py:25
  992.4 10.7 collective-permute-start.16
  996.3 9.0 copy-start.5
  996.9 8.4 copy-start.10
  998.0 13.5 %collective-permute-start.3 = (bf16[256,6,64]{0,2,1:T(8,128)(2,1)S(1)}, bf16[256,6,64]{0,2,1:T(8,128)(2,1)S(1)}, u32[]{:S(2)}, u32[]{:S(2)}) collective-permute-start(bf16[256,6,64]{0,2,1:T(8,128)(2,1)S(1)} %pad_maximum_fusion.2), channel_id=1, source_target_pairs={{0,4},{2,6},{4,0},{6,2},{8,12},{10,14},{12,8},{14,10},{16,20},{18,... | collective-permute-start | bytes 589832 | tf_op jit(solution)/shard_map/ppermute | solution.py:25
  998.9 2.3 copy-start.6
  999.6 23.7 %collective-permute-start.5 = (bf16[256,6,64]{0,2,1:T(8,128)(2,1)}, bf16[256,6,64]{0,2,1:T(8,128)(2,1)}, u32[]{:S(2)}, u32[]{:S(2)}) collective-permute-start(bf16[256,6,64]{0,2,1:T(8,128)(2,1)} %pad_maximum_fusion.3), channel_id=1, source_target_pairs={{0,4},{2,6},{4,0},{6,2},{8,12},{10,14},{12,8},{14,10},{16,20},{18,... | collective-permute-start | bytes 589832 | tf_op jit(solution)/shard_map/ppermute | solution.py:25
  1001.2 11.7 %collective-permute-start.13 = (bf16[256,6,64]{2,0,1:T(8,128)(2,1)S(1)}, bf16[256,6,64]{2,0,1:T(8,128)(2,1)S(1)}, u32[]{:S(2)}, u32[]{:S(2)}) collective-permute-start(bf16[256,6,64]{2,0,1:T(8,128)(2,1)S(1)} %pad_maximum_fusion), channel_id=1, source_target_pairs={{0,16},{2,18},{4,20},{6,22},{8,24},{10,26},{12,28},{14,30},{16,0},... | collective-permute-start | bytes 589832 | tf_op jit(solution)/shard_map/ppermute | solution.py:25
  1003.2 10.3 collective-permute-start.17
  1012.9 3.0 copy-start.3
  1013.0 1.9 copy-start.1
  1020.2 1.9 copy-start.2
  1022.6 1.4 copy-start.4
  1022.7 1.4 copy-start.7
  1022.7 1.4 copy-start.18
  1022.7 1.4 copy-start.19
Sparse Core Ops, SparseCore 0:
  1026.8 131.3 reduce-scatter.3
